TPU v7x, 256 devices: a whole 4x4x8 slice. The times are simulated.
256 devices in a mesh: dev: 256 (over z, y, x, core).
Axes of the slice: x: 4, y: 4, z: 8, core: 2. Of those that a mesh axis runs over, the one named last changes fastest.
Arguments:
- left_table: float32 [524288, 256], P('dev'), may hold values from -6 to 6
- left_state: float32 [524288], P('dev'), may hold values from 0.001 to 0.1
- right_table: float32 [524288, 256], P('dev'), may hold values from -6 to 6
- right_state: float32 [524288], P('dev'), may hold values from 0.001 to 0.1
- relations: float32 [4, 256, 256], replicated, may hold values from -0.375 to 0.375
- relation_state: float32 [4, 256], replicated, may hold values from 6553 to 655360
- edge_weights: int32 [256, 4, 16, 128, 128], P('dev'), may hold values from 0 to 3
- tile_left: int32 [256, 4, 16], P('dev'), may hold values from 0 to 15
- tile_right: int32 [256, 4, 16], P('dev'), may hold values from 0 to 15
- tile_relation: int32 [256, 4, 16], P('dev'), may hold values from 0 to 3
- live_count: int32 [256, 4], P('dev'), may hold values from 2 to 16, as said below
Outputs:
- left_out: float32 [524288, 256], P('dev')
- left_state_out: float32 [524288], P('dev')
- right_out: float32 [524288, 256], P('dev')
- right_state_out: float32 [524288], P('dev')
- relations_out: float32 [4, 256, 256], replicated
- relation_state_out: float32 [4, 256], replicated
Inputs may be any that keep to these rules, and one draw needn't show every extreme that they name: `live_count`: in round 0 some partition has exactly 16 live slots.
All inputs are finite; a program needn't handle non-finite values.
Results may differ from a plain program's by a relative error of at most 0.0003.
Values sent between devices are 32-bit elements; how exact they have to be, the bound alone decides.
A program may use at most 128 MiB of HBM per device.

v0:
```python
import functools
import jax
import jax.numpy as jnp
from jax import lax
from jax.experimental import pallas as pl
from jax.experimental.pallas import tpu as pltpu
from jax.sharding import Mesh
from jax.sharding import PartitionSpec as P

D = 256
TILE = 128
TILES = 16
ACTIVE = 16
RELS = 4
LEARN = 0.1
EPS = 1e-6
DEV = ("dev_0", "dev_1", "dev_2", "dev_3")
F32 = jnp.float32
BF16 = jnp.bfloat16


def halves(x):
    hi = x.astype(BF16)
    lo = (x - hi.astype(F32)).astype(BF16)
    return hi, lo


def product(a, b, dims):
    (ah, al), (bh, bl) = a, b
    (ca,), (cb,) = dims
    rows, depth = ah.shape
    if depth == TILE:
        lhs = jnp.concatenate([ah, al, ah], axis=ca)
        rhs = jnp.concatenate([bh, bh, bl], axis=cb)
        return lax.dot_general(lhs, rhs, (dims, ((), ())), preferred_element_type=F32)
    dot = functools.partial(
        lax.dot_general, dimension_numbers=(dims, ((), ())), preferred_element_type=F32
    )
    both = dot(jnp.concatenate([ah, al], axis=0), bh)
    return (both[:rows] + both[rows:]) + dot(ah, bl)


NN = ((1,), (0,))
NT = ((1,), (1,))


def round_kernel(
    turn,
    chained,
    in_place,
    lefts,
    rights,
    kinds,
    counts,
    lstate,
    rstate,
    left_in,
    right_in,
    relations,
    edges,
    *rest,
):
    if chained:
        rel_in, *rest = rest
    (
        left_out,
        lstate_out,
        right_out,
        rstate_out,
        rel_out,
        tl,
        tr,
        gl,
        gr,
        rg,
        mf,
        mh,
        ml,
        ew,
        stl,
        str_,
        hit,
        order,
        num,
        tsem,
        esem,
        msem,
        rsem,
        osem,
        ssem,
    ) = rest
    count = counts[turn]
    pairs = lax.div(count + 1, 2)
    tables = ((tl, left_in, left_out, lefts, gl), (tr, right_in, right_out, rights, gr))

    def tile_load(side, t):
        table, src, *_ = tables[side]
        rows = pl.ds(t * TILE, TILE)
        return pltpu.make_async_copy(src.at[rows, :], table.at[rows, :], tsem.at[side, t])

    def tile_store(side, t):
        table, _, dst, *_ = tables[side]
        rows = pl.ds(t * TILE, TILE)
        return pltpu.make_async_copy(table.at[rows, :], dst.at[rows, :], osem.at[side, t])

    def edge_copy(s):
        return pltpu.make_async_copy(edges.at[turn, s], ew.at[s], esem.at[s])

    rel_load = pltpu.make_async_copy(relations, mf, msem.at[0])
    rel_load.start()
    lines = pl.ds(0, TILES)
    states_in = [
        pltpu.make_async_copy(lstate, stl.at[lines, :], ssem.at[0]),
        pltpu.make_async_copy(rstate, str_.at[lines, :], ssem.at[1]),
    ]
    states_out = [
        pltpu.make_async_copy(stl.at[lines, :], lstate_out, ssem.at[2]),
        pltpu.make_async_copy(str_.at[lines, :], rstate_out, ssem.at[3]),
    ]
    for side in range(2):
        num[side] = 0
        for t in range(TILES):
            hit[side, t] = 0
            order[side, t] = TILES

    def mark(s, _):
        edge_copy(s).start()
        for side in range(2):
            t = tables[side][3][turn, s]

            @pl.when(hit[side, t] == 0)
            def _():
                tile_load(side, t).start()
                hit[side, t] = 1
                order[side, num[side]] = t
                num[side] = num[side] + 1

        return 0

    lax.fori_loop(0, 2 * pairs, mark, 0)
    for copy in states_in:
        copy.start()
    if chained:
        rg_load = pltpu.make_async_copy(rel_in, rg, rsem.at[0])
        rg_load.start()
    else:
        rg[...] = jnp.zeros_like(rg)

    def each_hit(side, act):
        def body(i, _):
            act(order[side, i])
            return 0

        lax.fori_loop(0, num[side], body, 0)

    def each_other(act):
        def body(t, _):
            for side in range(2):

                @pl.when(hit[side, t] == 0)
                def _():
                    act(side, t)

            return 0

        lax.fori_loop(0, TILES, body, 0)

    if not in_place:
        each_other(lambda side, t: tile_load(side, t).start())
    for side, (table, _, _, _, grad) in enumerate(tables):

        def clear(t):
            grad[pl.ds(t * TILE, TILE), :] = jnp.zeros((TILE, D), F32)

        each_hit(side, clear)
        spare = pl.ds(TILES * TILE, TILE)
        grad[spare, :] = jnp.zeros((TILE, D), F32)
        table[spare, :] = jnp.zeros((TILE, D), F32)
    for st in (stl, str_):
        st[pl.ds(TILES, 8), :] = jnp.zeros((8, TILE), F32)
    rel_load.wait()

    def split(r, _):
        hi, lo = halves(mf[r])
        mh[r] = hi
        ml[r] = lo
        return 0

    lax.fori_loop(0, RELS, split, 0)
    for side in range(2):
        each_hit(side, lambda t: tile_load(side, t).wait())
    for copy in states_in:
        copy.wait()
    if chained:
        rg_load.wait()

    def pair(i, _):
        slots = (2 * i, 2 * i + 1)
        for s in slots:
            edge_copy(s).wait()
        at = [lefts[turn, s] * TILE for s in slots]
        bt = [rights[turn, s] * TILE for s in slots]
        kd = [kinds[turn, s] for s in slots]
        live = [jnp.where(s < count, 1.0, 0.0).astype(F32) for s in slots]
        af = [tl[pl.ds(a, TILE), :] for a in at]
        a = [halves(x) for x in af]
        m = [(mh[k], ml[k]) for k in kd]
        p = [halves(product(x, y, NN)) for x, y in zip(a, m)]
        b = [halves(tr[pl.ds(x, TILE), :]) for x in bt]
        s_ = [product(x, y, NT) for x, y in zip(p, b)]
        g = []
        for s, sc, lv in zip(slots, s_, live):
            w = ew[s]
            zero = w == 0
            sc = sc * (D**-0.5)
            sig = jax.nn.sigmoid(jnp.where(zero, sc, -sc))
            coef = jnp.where(zero, 1.0, w.astype(F32) * (-1.0 / 3.0))
            g.append(sig * coef * (lv * D**-0.5))
        gs = [halves(x) for x in g]
        gts = [halves(x.T) for x in g]
        backed = [halves(product(x, y, NN)) for x, y in zip(gs, b)]
        tb = [product(x, y, NN) for x, y in zip(gts, p)]
        ta = [product(x, y, NT) for x, y in zip(backed, m)]
        ats = [halves(x.T) for x in af]
        tm = [product(x, y, NN) for x, y in zip(ats, backed)]
        for j in range(2):
            rows = pl.ds(bt[j], TILE)
            gr[rows, :] += tb[j]
        for j in range(2):
            rows = pl.ds(at[j], TILE)
            gl[rows, :] += ta[j]
        for j in range(2):
            rg[kd[j]] += tm[j]
        return 0

    lax.fori_loop(0, pairs, pair, 0)
    rg_store = pltpu.make_async_copy(rg, rel_out, rsem.at[1])
    rg_store.start()
    if not in_place:

        def pass_on(side, t):
            tile_load(side, t).wait()
            tile_store(side, t).start()

        each_other(pass_on)
    steps = jnp.maximum(num[0], num[1])

    def update(table, grad, st, t):
        rows = pl.ds(t * TILE, TILE)
        g = grad[rows, :]
        mean = jnp.sum(g * g, axis=1, keepdims=True) * (1.0 / D)
        wide = jnp.broadcast_to(st[pl.ds(t, 1), :], (TILE, TILE)).T + mean
        step = LEARN / (jnp.sqrt(wide) + EPS)
        new = table[rows, :] - g * jnp.concatenate([step, step], axis=1)
        return rows, new, wide.T[0:1, :]

    def finish(i, _):
        @pl.when(i < steps)
        def _():
            both = ((tl, gl, stl), (tr, gr, str_))
            at = [order[side, i] for side in range(2)]
            out = [update(*refs, t) for refs, t in zip(both, at)]
            for (table, _, st), t, (rows, new, line) in zip(both, at, out):
                table[rows, :] = new
                st[pl.ds(t, 1), :] = line

        before = jnp.maximum(i - 1, 0)
        for side in range(2):

            @pl.when((i > 0) & (before < num[side]))
            def _():
                tile_store(side, order[side, before]).start()

        return 0

    lax.fori_loop(0, steps + 1, finish, 0)
    for copy in states_out:
        copy.start()
    for side in range(2):
        each_hit(side, lambda t: tile_store(side, t).wait())
    if not in_place:
        each_other(lambda side, t: tile_store(side, t).wait())
    for copy in states_out:
        copy.wait()
    rg_store.wait()


def run_round(turn, ids, left, lstate, right, rstate, relations, edges, rel_grad):
    smem = pl.BlockSpec(memory_space=pltpu.SMEM)
    hbm = pl.BlockSpec(memory_space=pl.ANY)
    rows = TILES * TILE
    args = (*ids, lstate, rstate, left, right, relations, edges)
    specs = [smem] * 4 + [hbm] * 6
    chained = rel_grad is not None
    if chained:
        args += (rel_grad,)
        specs += [hbm]
    return pl.pallas_call(
        functools.partial(round_kernel, turn, chained, chained),
        name="bucket_round",
        out_shape=(
            jax.ShapeDtypeStruct((rows, D), F32),
            jax.ShapeDtypeStruct((TILES, TILE), F32),
            jax.ShapeDtypeStruct((rows, D), F32),
            jax.ShapeDtypeStruct((TILES, TILE), F32),
            jax.ShapeDtypeStruct((RELS, D, D), F32),
        ),
        in_specs=specs,
        out_specs=(hbm,) * 5,
        scratch_shapes=[
            pltpu.VMEM((rows + TILE, D), F32),
            pltpu.VMEM((rows + TILE, D), F32),
            pltpu.VMEM((rows + TILE, D), F32),
            pltpu.VMEM((rows + TILE, D), F32),
            pltpu.VMEM((RELS, D, D), F32),
            pltpu.VMEM((RELS, D, D), F32),
            pltpu.VMEM((RELS, D, D), BF16),
            pltpu.VMEM((RELS, D, D), BF16),
            pltpu.VMEM((ACTIVE, TILE, TILE), jnp.int32),
            pltpu.VMEM((TILES + 8, TILE), F32),
            pltpu.VMEM((TILES + 8, TILE), F32),
            pltpu.SMEM((2, TILES), jnp.int32),
            pltpu.SMEM((2, TILES), jnp.int32),
            pltpu.SMEM((2,), jnp.int32),
            pltpu.SemaphoreType.DMA((2, TILES)),
            pltpu.SemaphoreType.DMA((ACTIVE,)),
            pltpu.SemaphoreType.DMA((1,)),
            pltpu.SemaphoreType.DMA((2,)),
            pltpu.SemaphoreType.DMA((2, TILES)),
            pltpu.SemaphoreType.DMA((4,)),
        ],
        input_output_aliases={6: 0, 7: 2} if chained else {},
        compiler_params=pltpu.CompilerParams(vmem_limit_bytes=62 << 20),
        cost_estimate=pl.CostEstimate(
            flops=2_400_000_000, bytes_accessed=12_000_000, transcendentals=262144
        ),
    )(*args)


AXES = (("dev_0", 8), ("dev_1", 4), ("dev_2", 4), ("dev_3", 2))
PARTS = (6, 3, 2, 3, 2)
MESH = pl.DeviceIdType.MESH


def coordinates(index):
    z = lax.rem(lax.div(index, 32), 8)
    y = lax.rem(lax.div(index, 8), 4)
    x = lax.rem(lax.div(index, 2), 4)
    return (z, y, x, lax.rem(index, 2))


def home_kernel(
    back_left,
    back_right,
    left,
    lstate,
    right,
    rstate,
    grad,
    left_out,
    lstate_out,
    right_out,
    rstate_out,
    total,
    cbuf,
    xacc,
    xbuf,
    zacc,
    zbuf,
    ybuf,
    full,
    home_send,
    home_recv,
    csend,
    crecv,
    ysend,
    yrecv,
    zsend,
    zrecv,
    xsend,
    xrecv,
    tsem,
):
    z, y, x, c = (lax.axis_index(name) for name, _ in AXES)
    me = ((z * 4 + y) * 4 + x) * 2 + c
    count = 256

    def shifted_id(distance):
        return coordinates(lax.rem(me + count + distance, count))

    far = [(lax.rem(z + d, 8), y, x, c) for d in range(1, 8)]
    side = [(z, y, lax.rem(x + d, 4), c) for d in range(1, 4)]
    row = [(z, lax.rem(y + d, 4), x, c) for d in range(1, 4)]
    mate = (z, y, x, 1 - c)
    lines = [shifted_id(d) for d in (back_left, -back_left, back_right, -back_right)]
    peers = lines + [mate] + far + side + row
    barrier = pltpu.get_barrier_semaphore()
    for peer in peers:
        pl.semaphore_signal(barrier, inc=1, device_id=peer, device_id_type=MESH)
    pl.semaphore_wait(barrier, len(peers))

    def send(src, dst, ssem, rsem, peer):
        copy = pltpu.make_async_remote_copy(
            src_ref=src,
            dst_ref=dst,
            send_sem=ssem,
            recv_sem=rsem,
            device_id=peer,
            device_id_type=MESH,
        )
        copy.start()
        return copy

    half = 512
    copies = [
        send(
            grad.at[pl.ds((1 - c) * half, half), :], cbuf, csend.at[0], crecv.at[0], mate
        )
    ]
    homes = [
        send(rstate, rstate_out, home_send.at[0], home_recv.at[0], lines[2]),
        send(lstate, lstate_out, home_send.at[1], home_recv.at[1], lines[0]),
    ]

    def send_home(part):
        rows = pl.ds(sum(PARTS[:part]) * TILE, PARTS[part] * TILE)
        for i, (src, dst, peer) in enumerate(
            ((right, right_out, lines[2]), (left, left_out, lines[0]))
        ):
            at = 2 + 2 * part + i
            homes.append(
                send(src.at[rows, :], dst.at[rows, :], home_send.at[at], home_recv.at[at], peer)
            )

    copies[0].wait()

    def add_core(i, _):
        rows = pl.ds(i * TILE, TILE)
        part = pl.ds(lax.rem(i, 2) * TILE, TILE)
        xacc[lax.div(i, 2), part, :] = grad[pl.ds(c * half + i * TILE, TILE), :] + cbuf[rows, :]
        return 0

    lax.fori_loop(0, 4, add_core, 0)
    inner = (x == 1) | (x == 2)
    mine = lax.rem(x + 3, 4)

    def described(src, dst, ssem, rsem, peer):
        return pltpu.make_async_remote_copy(
            src_ref=src,
            dst_ref=dst,
            send_sem=ssem,
            recv_sem=rsem,
            device_id=peer,
            device_id_type=MESH,
        )

    def to_column(j):
        slot = lax.rem(x - j + 2, 4)
        return described(
            xacc.at[j], xbuf.at[slot], xsend.at[j], xrecv.at[slot], (z, y, 1 + j, c)
        )

    def from_row(slot):
        return described(xbuf.at[slot], xbuf.at[slot], xsend.at[0], xrecv.at[slot], side[0])

    for j in range(2):

        @pl.when(x != 1 + j)
        def _():
            to_column(j).start()

    send_home(0)
    for j in range(2):

        @pl.when(x != 1 + j)
        def _():
            to_column(j).wait_send()

    @pl.when(inner)
    def _():
        for slot in range(3):
            from_row(slot).wait_recv()

        def add_row(i, _):
            rows = pl.ds(i * 32, 32)
            zacc[i] = (xacc[mine, rows, :] + xbuf[0, rows, :]) + (
                xbuf[1, rows, :] + xbuf[2, rows, :]
            )
            return 0

        lax.fori_loop(0, 8, add_row, 0)
        for d, peer in enumerate(far):
            described(zacc.at[peer[0]], zbuf.at[d], zsend.at[d], zrecv.at[d], peer).start()

    send_home(1)

    @pl.when(inner)
    def _():
        for d, peer in enumerate(far):
            described(zacc.at[peer[0]], zbuf.at[d], zsend.at[d], zrecv.at[d], peer).wait()
        own = zacc[z]
        for d in range(7):
            own = own + zbuf[d]
        ybuf[y] = own
        for d, peer in enumerate(row):
            described(ybuf.at[y], ybuf.at[y], ysend.at[d], yrecv.at[d], peer).start()

    send_home(2)

    @pl.when(inner)
    def _():
        for d, peer in enumerate(row):
            described(ybuf.at[y], ybuf.at[y], ysend.at[d], yrecv.at[d], peer).wait()
        full[c, mine, z] = (ybuf[0] + ybuf[1]) + (ybuf[2] + ybuf[3])
        piece = full.at[c, mine, z]
        for d, peer in enumerate(far):
            described(piece, piece, zsend.at[7 + d], zrecv.at[7 + d], peer).start()

    send_home(3)

    def spread(j, d):
        piece = full.at[c, j]
        slot = 3 * j + d
        return described(piece, piece, xsend.at[2 + d], xrecv.at[3 + slot], (z, y, lax.rem(x + 1 + d, 4), c))

    @pl.when(inner)
    def _():
        piece = full.at[c, mine, z]
        for d, peer in enumerate(far):
            described(piece, piece, zsend.at[7 + d], zrecv.at[7 + d], peer).wait()
        for d in range(3):
            spread(mine, d).start()

    send_home(4)

    @pl.when(inner)
    def _():
        for d in range(3):
            spread(mine, d).wait_send()

    for j in range(2):

        @pl.when(x != 1 + j)
        def _():
            spread(j, lax.rem(x - j + 2, 4)).wait_recv()

    piece = full.at[c]
    send(piece, piece, csend.at[1], crecv.at[1], mate).wait()

    out = pltpu.make_async_copy(full, total, tsem.at[0])
    out.start()
    for copy in homes:
        copy.wait()
    out.wait()


def bring_home(back_left, back_right, left, lstate, right, rstate, grad):
    vmem = pl.BlockSpec(memory_space=pltpu.VMEM)
    hbm = pl.BlockSpec(memory_space=pl.ANY)
    like = lambda a: jax.ShapeDtypeStruct(a.shape, a.dtype)
    dma = pltpu.SemaphoreType.DMA
    return pl.pallas_call(
        functools.partial(home_kernel, back_left, back_right),
        name="bring_home",
        out_shape=tuple(like(a) for a in (left, lstate, right, rstate))
        + (jax.ShapeDtypeStruct((2, 2, 8, 32, D), F32),),
        in_specs=[hbm] * 4 + [vmem],
        out_specs=(hbm,) * 5,
        scratch_shapes=[
            pltpu.VMEM((512, D), F32),
            pltpu.VMEM((2, 256, D), F32),
            pltpu.VMEM((3, 256, D), F32),
            pltpu.VMEM((8, 32, D), F32),
            pltpu.VMEM((7, 32, D), F32),
            pltpu.VMEM((4, 32, D), F32),
            pltpu.VMEM((2, 2, 8, 32, D), F32),
            dma((12,)),
            dma((12,)),
            dma((2,)),
            dma((2,)),
            dma((3,)),
            dma((3,)),
            dma((14,)),
            dma((14,)),
            dma((5,)),
            dma((9,)),
            dma((1,)),
        ],
        compiler_params=pltpu.CompilerParams(
            collective_id=0, has_side_effects=True, vmem_limit_bytes=62 << 20
        ),
        cost_estimate=pl.CostEstimate(
            flops=2_000_000, bytes_accessed=12_000_000, transcendentals=1024
        ),
    )(left, lstate, right, rstate, grad)


def settle_kernel(
    left,
    lstate,
    right,
    rstate,
    total,
    rel,
    rel_state,
    left_out,
    lstate_out,
    right_out,
    rstate_out,
    rel_out,
    rel_state_out,
    tl,
    tr,
    sl,
    sr,
    grad,
    old,
    lines,
    isem,
    osem,
    gsem,
    rsem,
    ssem,
):
    parts = 8
    loads = [
        pltpu.make_async_copy(total, grad, gsem.at[0]),
        pltpu.make_async_copy(rel, old, gsem.at[1]),
    ]
    states = [
        pltpu.make_async_copy(lstate, sl, ssem.at[0]),
        pltpu.make_async_copy(rstate, sr, ssem.at[1]),
    ]
    states_back = [
        pltpu.make_async_copy(sl, lstate_out, ssem.at[2]),
        pltpu.make_async_copy(sr, rstate_out, ssem.at[3]),
    ]

    def table_in(side, i):
        rows = pl.ds(i * 256, 256)
        src, dst = ((left, tl), (right, tr))[side]
        return pltpu.make_async_copy(src.at[rows, :], dst.at[rows, :], isem.at[side, i])

    def table_out(side, i):
        rows = pl.ds(i * 256, 256)
        src, dst = ((tl, left_out), (tr, right_out))[side]
        return pltpu.make_async_copy(src.at[rows, :], dst.at[rows, :], osem.at[side, i])

    def rel_store(t):
        rows = pl.ds(t * TILE, TILE)
        return pltpu.make_async_copy(old.at[rows, :], rel_out.at[rows, :], rsem.at[t])

    for copy in loads + states:
        copy.start()

    def begin(i, _):
        table_in(0, i).start()
        table_in(1, i).start()
        return 0

    lax.fori_loop(0, parts, begin, 0)
    for t in range(parts):
        lines[t : t + 1, :] = rel_state[t // 2 : t // 2 + 1, (t % 2) * TILE : (t % 2 + 1) * TILE]
    for copy in loads:
        copy.wait()
    for copy, back in zip(states, states_back):
        copy.wait()
        back.start()

    def update(t, _):
        rows = pl.ds(t * TILE, TILE)
        g = grad[rows, :]
        mean = jnp.sum(g * g, axis=1, keepdims=True) * (1.0 / D)
        wide = jnp.broadcast_to(lines[pl.ds(t, 1), :], (TILE, TILE)).T + mean
        lines[pl.ds(t, 1), :] = wide.T[0:1, :]
        step = LEARN / (jnp.sqrt(wide) + EPS)
        old[rows, :] = old[rows, :] - g * jnp.concatenate([step, step], axis=1)
        for side in range(2):
            table_in(side, t).wait()
            table_out(side, t).start()

        @pl.when(t > 0)
        def _():
            rel_store(t - 1).start()

        return 0

    lax.fori_loop(0, parts, update, 0)
    for t in range(parts):
        rel_state_out[t // 2 : t // 2 + 1, (t % 2) * TILE : (t % 2 + 1) * TILE] = lines[t : t + 1, :]
    rel_store(parts - 1).start()

    def drain(i, _):
        table_out(0, i).wait()
        table_out(1, i).wait()
        rel_store(i).wait()
        return 0

    lax.fori_loop(0, parts, drain, 0)
    for back in states_back:
        back.wait()


def settle(left, lstate, right, rstate, total, rel, rel_state):
    vmem = pl.BlockSpec(memory_space=pltpu.VMEM)
    hbm = pl.BlockSpec(memory_space=pl.ANY)
    like = lambda a: jax.ShapeDtypeStruct(a.shape, a.dtype)
    dma = pltpu.SemaphoreType.DMA
    return pl.pallas_call(
        settle_kernel,
        name="settle",
        out_shape=tuple(like(a) for a in (left, lstate, right, rstate, rel, rel_state)),
        in_specs=[hbm] * 6 + [vmem],
        out_specs=(hbm,) * 5 + (vmem,),
        scratch_shapes=[
            pltpu.VMEM(left.shape, F32),
            pltpu.VMEM(right.shape, F32),
            pltpu.VMEM(lstate.shape, F32),
            pltpu.VMEM(rstate.shape, F32),
            pltpu.VMEM(rel.shape, F32),
            pltpu.VMEM(rel.shape, F32),
            pltpu.VMEM((8, TILE), F32),
            dma((2, 8)),
            dma((2, 8)),
            dma((2,)),
            dma((8,)),
            dma((4,)),
        ],
        compiler_params=pltpu.CompilerParams(vmem_limit_bytes=62 << 20),
        cost_estimate=pl.CostEstimate(
            flops=2_000_000, bytes_accessed=12_000_000, transcendentals=1024
        ),
    )(left, lstate, right, rstate, total, rel, rel_state)


def shifted(block, axis, distance):
    devices = range(lax.axis_size(axis))
    route = [((i - distance) % len(devices), i) for i in devices]
    return lax.ppermute(block, axis, route)


def per_device(
    left_table,
    left_state,
    right_table,
    right_state,
    relations,
    relation_state,
    edge_weights,
    tile_left,
    tile_right,
    tile_relation,
    live_count,
):
    edges = edge_weights[0]
    ids = (tile_left[0], tile_right[0], tile_relation[0], live_count[0])
    rounds = edges.shape[0]
    last = rounds - 1
    packed = jnp.concatenate([x[last].reshape(-1) for x in ids])
    last_edges, packed = shifted((edges[last:], packed), DEV, -1)
    rel_grad = None
    table_left, state_left = left_table, left_state.reshape(TILES, TILE)
    table_right, state_right = right_table, right_state.reshape(TILES, TILE)
    for turn in range(last):
        table_left, state_left, table_right, state_right, rel_grad = run_round(
            turn, ids, table_left, state_left, table_right, state_right, relations, edges, rel_grad
        )
        if turn + 1 < last:
            table_right, state_right = shifted((table_right, state_right), DEV, 1)
        if turn == 0:
            table_right, last_edges, packed = lax.optimization_barrier(
                (table_right, last_edges, packed)
            )
    last_ids = [packed[i * ACTIVE : (i + 1) * ACTIVE].reshape(1, ACTIVE) for i in range(3)]
    last_ids.append(packed[3 * ACTIVE :])
    table_left, state_left = shifted((table_left, state_left), DEV, -1)
    table_left, state_left, table_right, state_right, rel_grad = run_round(
        0, last_ids, table_left, state_left, table_right, state_right, relations, last_edges, rel_grad
    )
    kinds_count, width = (relations.shape[0], relations.shape[1])
    *home, total = bring_home(
        1,
        1 - last,
        table_left,
        state_left,
        table_right,
        state_right,
        rel_grad.reshape(kinds_count * width, width),
    )
    table_left, state_left, table_right, state_right, new_rel, new_state = settle(
        *home,
        total.reshape(kinds_count * width, width),
        relations.reshape(kinds_count * width, width),
        relation_state,
    )
    return (
        table_left,
        state_left.reshape(-1),
        table_right,
        state_right.reshape(-1),
        new_rel.reshape(kinds_count, width, width),
        new_state,
    )


def solution(mesh):
    torus = Mesh(mesh.devices.reshape(8, 4, 4, 2), ("dev_0", "dev_1", "dev_2", "dev_3"))
    return jax.shard_map(
        per_device,
        mesh=torus,
        in_specs=(
            P(DEV, None),
            P(DEV),
            P(DEV, None),
            P(DEV),
            P(),
            P(),
            P(DEV, None, None, None, None),
            P(DEV, None, None),
            P(DEV, None, None),
            P(DEV, None, None),
            P(DEV, None),
        ),
        out_specs=(P(DEV, None), P(DEV), P(DEV, None), P(DEV), P(), P()),
        check_vma=False,
    )
```

profile of v0, /device:TPU:58, one launch (start us, length us, event | category | flops | bytes accessed | tf_op | source)
XLA Modules:
  0.0 212.7 jit_solution(7685437618528730766)
XLA Ops:
  0.6 6.5 %bucket_round.4 = (f32[2048,256]{1,0:T(8,128)}, f32[16,128]{1,0:T(8,128)}, f32[2048,256]{1,0:T(8,128)}, f32[16,128]{1,0:T(8,128)}, f32[4,256,256]{2,1,0:T(8,128)}) custom-call(s32[4,16]{1,0:T(4,128)} %bitcast.40, s32[4,16]{1,0:T(4,128)} %bitcast.37, s32[4,16]{1,0:T(4,128)} %bitcast.34, s32[4]{0:T(128)} %bitcast.45, f32[16,128]{1,0:T(8,128)} %bitcast.43, ...), custom_call_target="tpu_custom_call" | custom-call | flops 2400000000 | bytes 12000000 | tf_op jit(solution)/shard_map/bucket_round/pallas_call | solution.py:298
  7.2 2.3 %collective-permute-start = (f32[2048,256]{1,0:T(8,128)}, f32[2048,256]{1,0:T(8,128)}, u32[]{:S(2)}, u32[]{:S(2)}) collective-permute-start(f32[2048,256]{1,0:T(8,128)} %get-tuple-element.40), channel_id=1, source_target_pairs={{255,0},{0,1},{1,2},{2,3},{3,4},{4,5},{5,6},{6,7},{7,8},{8,9},{9,1... | collective-permute-start | bytes 6291464 | tf_op jit(solution)/shard_map/ppermute | solution.py:739
  9.5 1.3 slice_bitcast_fusion
  11.5 0.6 slice.41
  12.1 0.7 slice_bitcast_fusion.6
  12.8 0.7 slice_bitcast_fusion.4
  13.5 0.7 pad_add_fusion
  14.2 1.3 collective-permute-start.2
  15.5 7.8 %collective-permute-done.2 = s32[49]{0:T(128)S(1)} collective-permute-done((s32[49]{0:T(128)S(1)}, s32[49]{0:T(128)S(1)}, u32[]{:S(2)}, u32[]{:S(2)}) %collective-permute-start.2) | collective-permute-done | bytes 228 | tf_op jit(solution)/shard_map/ppermute | solution.py:739
  23.3 9.8 %collective-permute-done.right_in = f32[2048,256]{1,0:T(8,128)} collective-permute-done((f32[2048,256]{1,0:T(8,128)}, f32[2048,256]{1,0:T(8,128)}, u32[]{:S(2)}, u32[]{:S(2)}) %collective-permute-start) | collective-permute-done | bytes 2097184 | tf_op jit(solution)/shard_map/ppermute | solution.py:739
  33.1 0.6 copy-done
  33.7 5.6 %bucket_round.5 = (f32[2048,256]{1,0:T(8,128)}, f32[16,128]{1,0:T(8,128)}, f32[2048,256]{1,0:T(8,128)}, f32[16,128]{1,0:T(8,128)}, f32[4,256,256]{2,1,0:T(8,128)}) custom-call(s32[4,16]{1,0:T(4,128)} %bitcast.41, s32[4,16]{1,0:T(4,128)} %bitcast.38, s32[4,16]{1,0:T(4,128)} %bitcast.35, s32[4]{0:T(128)} %bitcast.46, ...), custom_call_target="tpu_custom_call", output_to_operand_aliasing={{0}: (6, {}), {2}: (7, {})} | custom-call | flops 2400000000 | bytes 12000000 | tf_op jit(solution)/shard_map/bucket_round/pallas_call | solution.py:298
  39.3 5.2 %collective-permute-start.5 = (f32[2048,256]{1,0:T(8,128)}, f32[2048,256]{1,0:T(8,128)}, u32[]{:S(2)}, u32[]{:S(2)}) collective-permute-start(f32[2048,256]{1,0:T(8,128)} %get-tuple-element.50), channel_id=1, source_target_pairs={{255,0},{0,1},{1,2},{2,3},{3,4},{4,5},{5,6},{6,7},{7,8},{8,9},{9,1... | collective-permute-start | bytes 6291464 | tf_op jit(solution)/shard_map/ppermute | solution.py:739
  44.5 2.5 %collective-permute-start.4 = (f32[16,128]{1,0:T(8,128)}, f32[16,128]{1,0:T(8,128)S(1)}, u32[]{:S(2)}, u32[]{:S(2)}) collective-permute-start(f32[16,128]{1,0:T(8,128)} %get-tuple-element.48), channel_id=1, source_target_pairs={{255,0},{0,1},{1,2},{2,3},{3,4},{4,5},{5,6},{6,7},{7,8},{8,9},{9,1... | collective-permute-start | bytes 24584 | tf_op jit(solution)/shard_map/ppermute | solution.py:739
  47.0 18.2 %collective-permute-done.4.rstate = f32[16,128]{1,0:T(8,128)S(1)} collective-permute-done((f32[16,128]{1,0:T(8,128)}, f32[16,128]{1,0:T(8,128)S(1)}, u32[]{:S(2)}, u32[]{:S(2)}) %collective-permute-start.4) | collective-permute-done | bytes 8224 | tf_op jit(solution)/shard_map/ppermute | solution.py:739
  65.2 0.6 copy-done.1
  65.8 13.4 %bucket_round.6 = (f32[2048,256]{1,0:T(8,128)}, f32[16,128]{1,0:T(8,128)}, f32[2048,256]{1,0:T(8,128)}, f32[16,128]{1,0:T(8,128)}, f32[4,256,256]{2,1,0:T(8,128)}) custom-call(s32[4,16]{1,0:T(4,128)} %bitcast.42, s32[4,16]{1,0:T(4,128)} %bitcast.39, s32[4,16]{1,0:T(4,128)} %bitcast.36, s32[4]{0:T(128)} %bitcast.47, ...), custom_call_target="tpu_custom_call", output_to_operand_aliasing={{0}: (6, {}), {2}: (7, {})} | custom-call | flops 2400000000 | bytes 12000000 | tf_op jit(solution)/shard_map/bucket_round/pallas_call | solution.py:298
  79.3 3.1 %collective-permute-start.6 = (f32[16,128]{1,0:T(8,128)}, f32[16,128]{1,0:T(8,128)S(1)}, u32[]{:S(2)}, u32[]{:S(2)}) collective-permute-start(f32[16,128]{1,0:T(8,128)} %get-tuple-element.52), channel_id=1, source_target_pairs={{1,0},{2,1},{3,2},{4,3},{5,4},{6,5},{7,6},{8,7},{9,8},{10,9},{11,1... | collective-permute-start | bytes 24584 | tf_op jit(solution)/shard_map/ppermute | solution.py:739
  82.4 0.6 slice_bitcast_fusion.1
  83.5 19.6 %collective-permute-done.6.lstate = f32[16,128]{1,0:T(8,128)S(1)} collective-permute-done((f32[16,128]{1,0:T(8,128)}, f32[16,128]{1,0:T(8,128)S(1)}, u32[]{:S(2)}, u32[]{:S(2)}) %collective-permute-start.6) | collective-permute-done | bytes 8224 | tf_op jit(solution)/shard_map/ppermute | solution.py:739
  103.1 0.6 copy-done.5
  103.7 10.8 %bucket_round.7 = (f32[2048,256]{1,0:T(8,128)}, f32[16,128]{1,0:T(8,128)}, f32[2048,256]{1,0:T(8,128)}, f32[16,128]{1,0:T(8,128)}, f32[4,256,256]{2,1,0:T(8,128)}) custom-call(s32[1,16]{1,0:T(1,128)} %get-tuple-element.76.lefts, s32[1,16]{1,0:T(1,128)} %get-tuple-element.75.rights, ...), custom_call_target="tpu_custom_call", output_to_operand_aliasing={{0}: (6, {}), {2}: (7, {})} | custom-call | flops 2400000000 | bytes 12000000 | tf_op jit(solution)/shard_map/bucket_round/pallas_call | solution.py:298
  114.6 92.4 %bring_home.1 = (f32[2048,256]{1,0:T(8,128)}, f32[16,128]{1,0:T(8,128)}, f32[2048,256]{1,0:T(8,128)}, f32[16,128]{1,0:T(8,128)}, f32[2,2,8,32,256]{4,3,2,1,0:T(8,128)}) custom-call(f32[2048,256]{1,0:T(8,128)} %get-tuple-element.58.left, f32[16,128]{1,0:T(8,128)} %get-tuple-element.59.lstate, f32[2048,256]{1,0:T(8,128)} %get-tuple-element.60.right, ...), custom_call_target="tpu_custom_call" | custom-call | flops 2000000 | bytes 12000000 | tf_op jit(solution)/shard_map/bring_home/pallas_call | solution.py:562
  207.0 5.7 %settle.1 = (f32[2048,256]{1,0:T(8,128)}, f32[16,128]{1,0:T(8,128)}, f32[2048,256]{1,0:T(8,128)}, f32[16,128]{1,0:T(8,128)}, f32[1024,256]{1,0:T(8,128)}, /*index=5*/f32[4,256]{1,0:T(4,128)}) custom-call(f32[2048,256]{1,0:T(8,128)} %get-tuple-element.63.left, f32[16,128]{1,0:T(8,128)} %get-tuple-element.64.lstate, f32[2048,256]{1,0:T(8,128)} %get-tuple-element.65.right, ...), custom_call_target="tpu_custom_call" | custom-call | flops 2000000 | bytes 12000000 | tf_op jit(solution)/shard_map/settle/pallas_call | solution.py:709
  (17 shorter events, 1.3 us)
Async XLA Ops:
  7.2 3.8 %copy-start.4 = (f32[16,128]{1,0:T(8,128)S(1)}, f32[16,128]{1,0:T(8,128)}, u32[]{:S(2)}) copy-start(f32[16,128]{1,0:T(8,128)} %get-tuple-element.43) | copy-start | bytes 24580
  7.2 4.3 %copy-start.2 = (s32[1,4]{1,0:T(1,128)S(1)}, s32[1,4]{1,0:T(1,128)}, u32[]{:S(2)}) copy-start(s32[1,4]{1,0:T(1,128)} %param.21) | copy-start | bytes 52
  7.2 25.9 %collective-permute-start = (f32[2048,256]{1,0:T(8,128)}, f32[2048,256]{1,0:T(8,128)}, u32[]{:S(2)}, u32[]{:S(2)}) collective-permute-start(f32[2048,256]{1,0:T(8,128)} %get-tuple-element.40), channel_id=1, source_target_pairs={{255,0},{0,1},{1,2},{2,3},{3,4},{4,5},{5,6},{6,7},{7,8},{8,9},{9,1... | collective-permute-start | bytes 6291464 | tf_op jit(solution)/shard_map/ppermute | solution.py:739
  10.9 12.4 %collective-permute-start.1 = (s32[1,16,128,128]{3,2,1,0:T(8,128)S(1)}, s32[1,16,128,128]{3,2,1,0:T(8,128)S(1)}, u32[]{:S(2)}, u32[]{:S(2)}) collective-permute-start(s32[1,16,128,128]{3,2,1,0:T(8,128)S(1)} %slice_bitcast_fusion), channel_id=1, source_target_pairs={{1,0},{2,1},{3,2},{4,3},{5,4},{6,5},{7,6},{8,7},{9,8},{10,9},{11,1... | collective-permute-start | bytes 3145736 | tf_op jit(solution)/shard_map/ppermute | solution.py:739
  11.0 22.1 %collective-permute-start.3 = (f32[16,128]{1,0:T(8,128)S(1)}, f32[16,128]{1,0:T(8,128)S(1)}, u32[]{:S(2)}, u32[]{:S(2)}) collective-permute-start(f32[16,128]{1,0:T(8,128)S(1)} %copy-done.4), channel_id=1, source_target_pairs={{255,0},{0,1},{1,2},{2,3},{3,4},{4,5},{5,6},{6,7},{7,8},{8,9},{9,1... | collective-permute-start | bytes 24584 | tf_op jit(solution)/shard_map/ppermute | solution.py:739
  14.2 9.1 %collective-permute-start.2 = (s32[49]{0:T(128)S(1)}, s32[49]{0:T(128)S(1)}, u32[]{:S(2)}, u32[]{:S(2)}) collective-permute-start(s32[49]{0:T(128)S(1)} %pad_add_fusion), channel_id=1, source_target_pairs={{1,0},{2,1},{3,2},{4,3},{5,4},{6,5},{7,6},{8,7},{9,8},{10,9},{11,1... | collective-permute-start | bytes 596 | tf_op jit(solution)/shard_map/ppermute | solution.py:739
  23.3 55.9 %copy-start.3 = (s32[1,16,128,128]{3,2,1,0:T(8,128)}, s32[1,16,128,128]{3,2,1,0:T(8,128)S(1)}, u32[]{:S(2)}) copy-start(s32[1,16,128,128]{3,2,1,0:T(8,128)S(1)} %collective-permute-done.1.edges) | copy-start | bytes 3145732
  33.1 0.6 copy-start
  39.3 25.9 %collective-permute-start.5 = (f32[2048,256]{1,0:T(8,128)}, f32[2048,256]{1,0:T(8,128)}, u32[]{:S(2)}, u32[]{:S(2)}) collective-permute-start(f32[2048,256]{1,0:T(8,128)} %get-tuple-element.50), channel_id=1, source_target_pairs={{255,0},{0,1},{1,2},{2,3},{3,4},{4,5},{5,6},{6,7},{7,8},{8,9},{9,1... | collective-permute-start | bytes 6291464 | tf_op jit(solution)/shard_map/ppermute | solution.py:739
  44.5 20.7 %collective-permute-start.4 = (f32[16,128]{1,0:T(8,128)}, f32[16,128]{1,0:T(8,128)S(1)}, u32[]{:S(2)}, u32[]{:S(2)}) collective-permute-start(f32[16,128]{1,0:T(8,128)} %get-tuple-element.48), channel_id=1, source_target_pairs={{255,0},{0,1},{1,2},{2,3},{3,4},{4,5},{5,6},{6,7},{7,8},{8,9},{9,1... | collective-permute-start | bytes 24584 | tf_op jit(solution)/shard_map/ppermute | solution.py:739
  65.2 0.6 copy-start.1
  79.2 24.0 %collective-permute-start.7 = (f32[2048,256]{1,0:T(8,128)}, f32[2048,256]{1,0:T(8,128)}, u32[]{:S(2)}, u32[]{:S(2)}) collective-permute-start(f32[2048,256]{1,0:T(8,128)} %get-tuple-element.54), channel_id=1, source_target_pairs={{1,0},{2,1},{3,2},{4,3},{5,4},{6,5},{7,6},{8,7},{9,8},{10,9},{11,1... | collective-permute-start | bytes 6291464 | tf_op jit(solution)/shard_map/ppermute | solution.py:739
  79.3 23.9 %collective-permute-start.6 = (f32[16,128]{1,0:T(8,128)}, f32[16,128]{1,0:T(8,128)S(1)}, u32[]{:S(2)}, u32[]{:S(2)}) collective-permute-start(f32[16,128]{1,0:T(8,128)} %get-tuple-element.52), channel_id=1, source_target_pairs={{1,0},{2,1},{3,2},{4,3},{5,4},{6,5},{7,6},{8,7},{9,8},{10,9},{11,1... | collective-permute-start | bytes 24584 | tf_op jit(solution)/shard_map/ppermute | solution.py:739
  103.1 0.6 copy-start.5
where the time goes:
time: 215 us; the launch traced here: 213 us
  Pallas kernels  135 us (63%)
  waiting for transfers between devices  55.4 us (26%)
  starting transfers between devices  15.1 us (7%)
  local copies, waits for them, and re-layouts  6.24 us (3%)
    pallas_call x1, Pallas kernels, bring_home(): pl.pallas_call(functools.partial(home_kernel, back_left, back_right), nam...  92.4 us
    ppermute x8, waiting for transfers between devices, shifted(): return lax.ppermute(block, axis, route)  55.4 us
    pallas_call x4, Pallas kernels, run_round(): pl.pallas_call(functools.partial(round_kernel, turn, chained, chained), n...  36.4 us
    ppermute x8, starting transfers between devices, shifted(): return lax.ppermute(block, axis, route)  15.1 us
    pallas_call x1, Pallas kernels, settle(): pl.pallas_call(settle_kernel, name='settle', out_shape=tuple((like(a) for...  5.75 us
  transfers between devices with their start and end apart: 8, of which 4 were waited for; matrix products, arithmetic and copies ran while one was open for 2% of the time, Pallas kernels for 0%

commit v1 on v0

--- a/solution.py
+++ b/solution.py
@@ -338,7 +338,7 @@
 
 
 AXES = (("dev_0", 8), ("dev_1", 4), ("dev_2", 4), ("dev_3", 2))
-PARTS = (6, 3, 2, 3, 2)
+PARTS = (2, 3, 3, 2, 3, 3)
 MESH = pl.DeviceIdType.MESH
 
 
@@ -432,6 +432,7 @@
                 send(src.at[rows, :], dst.at[rows, :], home_send.at[at], home_recv.at[at], peer)
             )
 
+    send_home(0)
     copies[0].wait()
 
     def add_core(i, _):
@@ -469,13 +470,7 @@
         def _():
             to_column(j).start()
 
-    send_home(0)
-    for j in range(2):
-
-        @pl.when(x != 1 + j)
-        def _():
-            to_column(j).wait_send()
-
+    send_home(1)
     @pl.when(inner)
     def _():
         for slot in range(3):
@@ -492,7 +487,7 @@
         for d, peer in enumerate(far):
             described(zacc.at[peer[0]], zbuf.at[d], zsend.at[d], zrecv.at[d], peer).start()
 
-    send_home(1)
+    send_home(2)
 
     @pl.when(inner)
     def _():
@@ -505,7 +500,7 @@
         for d, peer in enumerate(row):
             described(ybuf.at[y], ybuf.at[y], ysend.at[d], yrecv.at[d], peer).start()
 
-    send_home(2)
+    send_home(3)
 
     @pl.when(inner)
     def _():
@@ -516,7 +511,7 @@
         for d, peer in enumerate(far):
             described(piece, piece, zsend.at[7 + d], zrecv.at[7 + d], peer).start()
 
-    send_home(3)
+    send_home(4)
 
     def spread(j, d):
         piece = full.at[c, j]
@@ -531,21 +526,27 @@
         for d in range(3):
             spread(mine, d).start()
 
-    send_home(4)
+    send_home(5)
+
+    for j in range(2):
+
+        @pl.when(x != 1 + j)
+        def _():
+            spread(j, lax.rem(x - j + 2, 4)).wait_recv()
+
+    piece = full.at[c]
+    send(piece, piece, csend.at[1], crecv.at[1], mate).wait()
+    for j in range(2):
+
+        @pl.when(x != 1 + j)
+        def _():
+            to_column(j).wait_send()
 
     @pl.when(inner)
     def _():
         for d in range(3):
             spread(mine, d).wait_send()
 
-    for j in range(2):
-
-        @pl.when(x != 1 + j)
-        def _():
-            spread(j, lax.rem(x - j + 2, 4)).wait_recv()
-
-    piece = full.at[c]
-    send(piece, piece, csend.at[1], crecv.at[1], mate).wait()
 
     out = pltpu.make_async_copy(full, total, tsem.at[0])
     out.start()
@@ -574,8 +575,8 @@
             pltpu.VMEM((7, 32, D), F32),
             pltpu.VMEM((4, 32, D), F32),
             pltpu.VMEM((2, 2, 8, 32, D), F32),
-            dma((12,)),
-            dma((12,)),
+            dma((14,)),
+            dma((14,)),
             dma((2,)),
             dma((2,)),
             dma((3,)),

time: 215 us -> 209 us (0.972)
  Pallas kernels: 135 us -> 129 us
  starting transfers between devices: 15.1 us -> 10.6 us
  waiting for transfers between devices: 55.4 us -> 59.9 us
    pallas_call x1, Pallas kernels: 92.4 us -> 85.6 us  [bring_home(): pl.pallas_call(functools.partial(home_kernel, back_left, back_right), nam...]
    ppermute x8, starting transfers between devices: 15.1 us -> 10.6 us  [shifted(): return lax.ppermute(block, axis, route)]
    ppermute x8, waiting for transfers between devices: 55.4 us -> 59.9 us  [shifted(): return lax.ppermute(block, axis, route)]
where the time goes in v1:
time: 209 us; the launch traced here: 207 us
  Pallas kernels  129 us (62%)
  waiting for transfers between devices  59.9 us (29%)
  starting transfers between devices  10.6 us (5%)
  local copies, waits for them, and re-layouts  6.24 us (3%)
    pallas_call x1, Pallas kernels, bring_home(): pl.pallas_call(functools.partial(home_kernel, back_left, back_right), nam...  85.6 us
    ppermute x8, waiting for transfers between devices, shifted(): return lax.ppermute(block, axis, route)  59.9 us
    pallas_call x4, Pallas kernels, run_round(): pl.pallas_call(functools.partial(round_kernel, turn, chained, chained), n...  37.8 us
    ppermute x8, starting transfers between devices, shifted(): return lax.ppermute(block, axis, route)  10.6 us
    pallas_call x1, Pallas kernels, settle(): pl.pallas_call(settle_kernel, name='settle', out_shape=tuple((like(a) for...  5.75 us
  transfers between devices with their start and end apart: 8, of which 4 were waited for; matrix products, arithmetic and copies ran while one was open for 2% of the time, Pallas kernels for 0%

profile of v1, /device:TPU:58, one launch (start us, length us, event | category | flops | bytes accessed | tf_op | source)
XLA Modules:
  0.0 207.3 jit_solution(10046929998167427458)
XLA Ops:
  0.6 10.5 %bucket_round.4 = (f32[2048,256]{1,0:T(8,128)}, f32[16,128]{1,0:T(8,128)}, f32[2048,256]{1,0:T(8,128)}, f32[16,128]{1,0:T(8,128)}, f32[4,256,256]{2,1,0:T(8,128)}) custom-call(s32[4,16]{1,0:T(4,128)} %bitcast.40, s32[4,16]{1,0:T(4,128)} %bitcast.37, s32[4,16]{1,0:T(4,128)} %bitcast.34, s32[4]{0:T(128)} %bitcast.45, f32[16,128]{1,0:T(8,128)} %bitcast.43, ...), custom_call_target="tpu_custom_call" | custom-call | flops 2400000000 | bytes 12000000 | tf_op jit(solution)/shard_map/bucket_round/pallas_call | solution.py:298
  11.2 0.3 collective-permute-start
  11.5 1.3 slice_bitcast_fusion
  12.8 1.6 collective-permute-start.1
  14.4 1.8 collective-permute-start.3
  16.2 0.6 slice.41
  16.8 0.7 slice_bitcast_fusion.6
  17.5 0.7 slice_bitcast_fusion.4
  18.2 0.7 pad_add_fusion
  18.9 7.8 %collective-permute-done.2 = s32[49]{0:T(128)S(1)} collective-permute-done((s32[49]{0:T(128)S(1)}, s32[49]{0:T(128)S(1)}, u32[]{:S(2)}, u32[]{:S(2)}) %collective-permute-start.2) | collective-permute-done | bytes 228 | tf_op jit(solution)/shard_map/ppermute | solution.py:740
  26.7 10.3 %collective-permute-done.right_in = f32[2048,256]{1,0:T(8,128)} collective-permute-done((f32[2048,256]{1,0:T(8,128)}, f32[2048,256]{1,0:T(8,128)}, u32[]{:S(2)}, u32[]{:S(2)}) %collective-permute-start) | collective-permute-done | bytes 2097184 | tf_op jit(solution)/shard_map/ppermute | solution.py:740
  37.0 0.6 copy-done
  37.6 13.9 %bucket_round.5 = (f32[2048,256]{1,0:T(8,128)}, f32[16,128]{1,0:T(8,128)}, f32[2048,256]{1,0:T(8,128)}, f32[16,128]{1,0:T(8,128)}, f32[4,256,256]{2,1,0:T(8,128)}) custom-call(s32[4,16]{1,0:T(4,128)} %bitcast.41, s32[4,16]{1,0:T(4,128)} %bitcast.38, s32[4,16]{1,0:T(4,128)} %bitcast.35, s32[4]{0:T(128)} %bitcast.46, ...), custom_call_target="tpu_custom_call", output_to_operand_aliasing={{0}: (6, {}), {2}: (7, {})} | custom-call | flops 2400000000 | bytes 12000000 | tf_op jit(solution)/shard_map/bucket_round/pallas_call | solution.py:298
  51.7 25.7 %collective-permute-done.4.rstate = f32[16,128]{1,0:T(8,128)S(1)} collective-permute-done((f32[16,128]{1,0:T(8,128)}, f32[16,128]{1,0:T(8,128)S(1)}, u32[]{:S(2)}, u32[]{:S(2)}) %collective-permute-start.4) | collective-permute-done | bytes 8224 | tf_op jit(solution)/shard_map/ppermute | solution.py:740
  77.4 0.6 copy-done.1
  78.0 7.4 %bucket_round.6 = (f32[2048,256]{1,0:T(8,128)}, f32[16,128]{1,0:T(8,128)}, f32[2048,256]{1,0:T(8,128)}, f32[16,128]{1,0:T(8,128)}, f32[4,256,256]{2,1,0:T(8,128)}) custom-call(s32[4,16]{1,0:T(4,128)} %bitcast.42, s32[4,16]{1,0:T(4,128)} %bitcast.39, s32[4,16]{1,0:T(4,128)} %bitcast.36, s32[4]{0:T(128)} %bitcast.47, ...), custom_call_target="tpu_custom_call", output_to_operand_aliasing={{0}: (6, {}), {2}: (7, {})} | custom-call | flops 2400000000 | bytes 12000000 | tf_op jit(solution)/shard_map/bucket_round/pallas_call | solution.py:298
  85.4 6.6 %collective-permute-start.6 = (f32[16,128]{1,0:T(8,128)}, f32[16,128]{1,0:T(8,128)S(1)}, u32[]{:S(2)}, u32[]{:S(2)}) collective-permute-start(f32[16,128]{1,0:T(8,128)} %get-tuple-element.52), channel_id=1, source_target_pairs={{1,0},{2,1},{3,2},{4,3},{5,4},{6,5},{7,6},{8,7},{9,8},{10,9},{11,1... | collective-permute-start | bytes 24584 | tf_op jit(solution)/shard_map/ppermute | solution.py:740
  92.0 0.6 slice_bitcast_fusion.1
  92.6 0.6 slice.46.counts
  93.2 16.1 %collective-permute-done.6.lstate = f32[16,128]{1,0:T(8,128)S(1)} collective-permute-done((f32[16,128]{1,0:T(8,128)}, f32[16,128]{1,0:T(8,128)S(1)}, u32[]{:S(2)}, u32[]{:S(2)}) %collective-permute-start.6) | collective-permute-done | bytes 8224 | tf_op jit(solution)/shard_map/ppermute | solution.py:740
  109.3 0.6 copy-done.5
  109.9 6.1 %bucket_round.7 = (f32[2048,256]{1,0:T(8,128)}, f32[16,128]{1,0:T(8,128)}, f32[2048,256]{1,0:T(8,128)}, f32[16,128]{1,0:T(8,128)}, f32[4,256,256]{2,1,0:T(8,128)}) custom-call(s32[1,16]{1,0:T(1,128)} %get-tuple-element.76.lefts, s32[1,16]{1,0:T(1,128)} %get-tuple-element.75.rights, ...), custom_call_target="tpu_custom_call", output_to_operand_aliasing={{0}: (6, {}), {2}: (7, {})} | custom-call | flops 2400000000 | bytes 12000000 | tf_op jit(solution)/shard_map/bucket_round/pallas_call | solution.py:298
  115.9 85.6 %bring_home.1 = (f32[2048,256]{1,0:T(8,128)}, f32[16,128]{1,0:T(8,128)}, f32[2048,256]{1,0:T(8,128)}, f32[16,128]{1,0:T(8,128)}, f32[2,2,8,32,256]{4,3,2,1,0:T(8,128)}) custom-call(f32[2048,256]{1,0:T(8,128)} %get-tuple-element.58.left, f32[16,128]{1,0:T(8,128)} %get-tuple-element.59.lstate, f32[2048,256]{1,0:T(8,128)} %get-tuple-element.60.right, ...), custom_call_target="tpu_custom_call" | custom-call | flops 2000000 | bytes 12000000 | tf_op jit(solution)/shard_map/bring_home/pallas_call | solution.py:563
  201.6 5.7 %settle.1 = (f32[2048,256]{1,0:T(8,128)}, f32[16,128]{1,0:T(8,128)}, f32[2048,256]{1,0:T(8,128)}, f32[16,128]{1,0:T(8,128)}, f32[1024,256]{1,0:T(8,128)}, /*index=5*/f32[4,256]{1,0:T(4,128)}) custom-call(f32[2048,256]{1,0:T(8,128)} %get-tuple-element.63.left, f32[16,128]{1,0:T(8,128)} %get-tuple-element.64.lstate, f32[2048,256]{1,0:T(8,128)} %get-tuple-element.65.right, ...), custom_call_target="tpu_custom_call" | custom-call | flops 2000000 | bytes 12000000 | tf_op jit(solution)/shard_map/settle/pallas_call | solution.py:710
  (17 shorter events, 0.3 us)
Async XLA Ops:
  11.1 3.3 %copy-start.4 = (f32[16,128]{1,0:T(8,128)S(1)}, f32[16,128]{1,0:T(8,128)}, u32[]{:S(2)}) copy-start(f32[16,128]{1,0:T(8,128)} %get-tuple-element.43) | copy-start | bytes 24580
  11.1 5.1 %copy-start.2 = (s32[1,4]{1,0:T(1,128)S(1)}, s32[1,4]{1,0:T(1,128)}, u32[]{:S(2)}) copy-start(s32[1,4]{1,0:T(1,128)} %param.21) | copy-start | bytes 52
  11.2 25.9 %collective-permute-start = (f32[2048,256]{1,0:T(8,128)}, f32[2048,256]{1,0:T(8,128)}, u32[]{:S(2)}, u32[]{:S(2)}) collective-permute-start(f32[2048,256]{1,0:T(8,128)} %get-tuple-element.40), channel_id=1, source_target_pairs={{255,0},{0,1},{1,2},{2,3},{3,4},{4,5},{5,6},{6,7},{7,8},{8,9},{9,1... | collective-permute-start | bytes 6291464 | tf_op jit(solution)/shard_map/ppermute | solution.py:740
  12.8 14.0 %collective-permute-start.1 = (s32[1,16,128,128]{3,2,1,0:T(8,128)S(1)}, s32[1,16,128,128]{3,2,1,0:T(8,128)S(1)}, u32[]{:S(2)}, u32[]{:S(2)}) collective-permute-start(s32[1,16,128,128]{3,2,1,0:T(8,128)S(1)} %slice_bitcast_fusion), channel_id=1, source_target_pairs={{1,0},{2,1},{3,2},{4,3},{5,4},{6,5},{7,6},{8,7},{9,8},{10,9},{11,1... | collective-permute-start | bytes 3145736 | tf_op jit(solution)/shard_map/ppermute | solution.py:740
  14.4 22.6 %collective-permute-start.3 = (f32[16,128]{1,0:T(8,128)S(1)}, f32[16,128]{1,0:T(8,128)S(1)}, u32[]{:S(2)}, u32[]{:S(2)}) collective-permute-start(f32[16,128]{1,0:T(8,128)S(1)} %copy-done.4), channel_id=1, source_target_pairs={{255,0},{0,1},{1,2},{2,3},{3,4},{4,5},{5,6},{6,7},{7,8},{8,9},{9,1... | collective-permute-start | bytes 24584 | tf_op jit(solution)/shard_map/ppermute | solution.py:740
  18.9 7.8 %collective-permute-start.2 = (s32[49]{0:T(128)S(1)}, s32[49]{0:T(128)S(1)}, u32[]{:S(2)}, u32[]{:S(2)}) collective-permute-start(s32[49]{0:T(128)S(1)} %pad_add_fusion), channel_id=1, source_target_pairs={{1,0},{2,1},{3,2},{4,3},{5,4},{6,5},{7,6},{8,7},{9,8},{10,9},{11,1... | collective-permute-start | bytes 596 | tf_op jit(solution)/shard_map/ppermute | solution.py:740
  26.7 58.6 %copy-start.3 = (s32[1,16,128,128]{3,2,1,0:T(8,128)}, s32[1,16,128,128]{3,2,1,0:T(8,128)S(1)}, u32[]{:S(2)}) copy-start(s32[1,16,128,128]{3,2,1,0:T(8,128)S(1)} %collective-permute-done.1.edges) | copy-start | bytes 3145732
  37.0 0.6 copy-start
  51.5 25.9 %collective-permute-start.5 = (f32[2048,256]{1,0:T(8,128)}, f32[2048,256]{1,0:T(8,128)}, u32[]{:S(2)}, u32[]{:S(2)}) collective-permute-start(f32[2048,256]{1,0:T(8,128)} %get-tuple-element.50), channel_id=1, source_target_pairs={{255,0},{0,1},{1,2},{2,3},{3,4},{4,5},{5,6},{6,7},{7,8},{8,9},{9,1... | collective-permute-start | bytes 6291464 | tf_op jit(solution)/shard_map/ppermute | solution.py:740
  51.6 25.8 %collective-permute-start.4 = (f32[16,128]{1,0:T(8,128)}, f32[16,128]{1,0:T(8,128)S(1)}, u32[]{:S(2)}, u32[]{:S(2)}) collective-permute-start(f32[16,128]{1,0:T(8,128)} %get-tuple-element.48), channel_id=1, source_target_pairs={{255,0},{0,1},{1,2},{2,3},{3,4},{4,5},{5,6},{6,7},{7,8},{8,9},{9,1... | collective-permute-start | bytes 24584 | tf_op jit(solution)/shard_map/ppermute | solution.py:740
  77.4 0.6 copy-start.1
  85.3 24.0 %collective-permute-start.7 = (f32[2048,256]{1,0:T(8,128)}, f32[2048,256]{1,0:T(8,128)}, u32[]{:S(2)}, u32[]{:S(2)}) collective-permute-start(f32[2048,256]{1,0:T(8,128)} %get-tuple-element.54), channel_id=1, source_target_pairs={{1,0},{2,1},{3,2},{4,3},{5,4},{6,5},{7,6},{8,7},{9,8},{10,9},{11,1... | collective-permute-start | bytes 6291464 | tf_op jit(solution)/shard_map/ppermute | solution.py:740
  85.4 23.9 %collective-permute-start.6 = (f32[16,128]{1,0:T(8,128)}, f32[16,128]{1,0:T(8,128)S(1)}, u32[]{:S(2)}, u32[]{:S(2)}) collective-permute-start(f32[16,128]{1,0:T(8,128)} %get-tuple-element.52), channel_id=1, source_target_pairs={{1,0},{2,1},{3,2},{4,3},{5,4},{6,5},{7,6},{8,7},{9,8},{10,9},{11,1... | collective-permute-start | bytes 24584 | tf_op jit(solution)/shard_map/ppermute | solution.py:740
  109.3 0.6 copy-start.5
